TPU v7x, 256 devices: a whole 4x4x8 slice. The times are simulated.
256 devices in a mesh: slab: 64 (over x_lo, y, z), subj: 2 (over core), tm: 2 (over x_hi).
Axes of the slice: x: 4 (x_hi: 2, x_lo: 2; x = x_hi * 2 + x_lo), y: 4, z: 8, core: 2. Of those that a mesh axis runs over, the one named last changes fastest.
Arguments:
- subject_data: bfloat16 [2, 128, 128, 2048], P('subj', 'slab', None, 'tm'), may hold values from -8 to 8
- template: bfloat16 [128, 128, 2048], P('slab', None, 'tm'), may hold values from -8 to 8
- neighbours: int32 [128, 27], P('slab'), may hold values from 0 to 127, as said below
- valid: int32 [128, 27], P('slab'), may hold values from 0 to 1, as said below
Outputs:
- new_template: bfloat16 [128, 128, 2048], P('slab', None, 'tm')
Inputs may be any that keep to these rules, and one draw needn't show every extreme that they name: `neighbours`: slots 9 l to 9 l + 8 of block b name blocks of the slab of b shifted by l - 1 (slabs hold 2 consecutive blocks); where that slab doesn't exist they name b itself. Slot 13 names b itself. `valid`: slot 13 is always 1; slots whose slab doesn't exist are 0.
All inputs are finite; a program needn't handle non-finite values.
Results may differ from a plain program's by a relative error of at most 0.007.
Values may be sent and summed in bfloat16 or wider, within the bound.
A program may use at most 64 MiB of HBM per device.

v0:
```python
import jax
import jax.numpy as jnp
from jax import lax
from jax.sharding import PartitionSpec as P

ITERS = 3


def from_everyone(x, axis):
    size = lax.axis_size(axis)
    return lax.all_to_all(jnp.broadcast_to(x[None], (size, *x.shape)), axis, 0, 0, tiled=True)


def over_copies(x, axis):
    everything = from_everyone(x, axis)
    return jnp.sum(everything, axis=0)


def laid_out(pieces, dim):
    pieces = jnp.moveaxis(pieces, 0, dim)
    lengths = pieces.shape
    return pieces.reshape(*lengths[:dim], lengths[dim] * lengths[dim + 1], *lengths[dim + 2 :])


def gather_directly(x, axis, dim):
    return laid_out(from_everyone(x, axis), dim)


def with_halo(cells, sides, width):
    for axis, dim in sides:
        count = lax.axis_size(axis)
        ends = count - 1
        head = lax.slice_in_dim(cells, 0, width, axis=dim)
        tail = lax.slice_in_dim(cells, cells.shape[dim] - width, cells.shape[dim], axis=dim)
        cells = jnp.concatenate(
            [
                lax.ppermute(tail, axis, [(i, (i + 1) % count) for i in range(ends)]),
                cells,
                lax.ppermute(head, axis, [((i + 1) % count, i) for i in range(ends)]),
            ],
            axis=dim,
        )
    return cells


def split_up(x, dim, size):
    before, after = (x.shape[:dim], x.shape[dim + 1 :])
    return jnp.moveaxis(x.reshape(*before, size, -1, *after), dim, 0)


def edges_of(length, count):
    unit = 8 if length >= 8 * count else 1
    return [length // unit * k // count * unit for k in range(1, count)]


def exchange_in_pieces(x, axis, pieces, split_dim, concat_dim):
    blocks = split_up(x, split_dim, lax.axis_size(axis))
    cut = max(range(1, max(2, blocks.ndim - 1)), key=lambda d: blocks.shape[d])
    gathered = []
    for piece in jnp.split(blocks, edges_of(blocks.shape[cut], pieces), axis=cut):
        if piece.size:
            gathered.append(lax.all_to_all(piece, axis, split_axis=0, concat_axis=0, tiled=True))
    return laid_out(jnp.concatenate(gathered, axis=cut), concat_dim)


def balance(cross, row_norm, col_norm, mask):
    width = cross.shape[-1]
    logits = cross * row_norm[None, :, None, None] * col_norm[:, None, :, :] / 0.03
    masked = mask[None, None, :, None]
    kernel = jnp.exp(logits) * masked
    target = masked / (width * jnp.sum(mask))
    filler = 1.0 - masked
    col_weight = jnp.ones((cross.shape[0], 1, cross.shape[2], width), jnp.float32)
    for step in range(ITERS):
        row_weight = 1.0 / width / jnp.sum(kernel * col_weight, axis=(2, 3), keepdims=True)
        col_weight = target / (jnp.sum(kernel * row_weight, axis=1, keepdims=True) + filler)
    flow = kernel * col_weight
    return (flow / jnp.sum(flow, axis=(2, 3), keepdims=True)).astype(jnp.bfloat16)


def square_sum(values):
    return jnp.einsum("...t,...t->...", values, values, preferred_element_type=jnp.float32)


def slot_cross(tmpl_block, extended, slots):
    whole = jnp.einsum("it,sejt->siej", tmpl_block, extended, preferred_element_type=jnp.float32)
    return jnp.take(whole, slots, axis=2)


def project(plan, extended, slots):
    places = (slots[:, None] == jnp.arange(extended.shape[1], dtype=jnp.int32)[None, :]).astype(
        jnp.float32
    )
    folded = jnp.einsum(
        "sikj,ke->siej", plan.astype(jnp.float32), places, precision=lax.Precision.HIGHEST
    )
    upper = folded.astype(jnp.bfloat16)
    lower = (folded - upper.astype(jnp.float32)).astype(jnp.bfloat16)
    total = jnp.einsum("siej,sejt->it", upper, extended, preferred_element_type=jnp.float32)
    return total + jnp.einsum("siej,sejt->it", lower, extended, preferred_element_type=jnp.float32)


def subject_mean(moved, count):
    total = over_copies(moved, "subj")
    return (total / count).astype(jnp.bfloat16)


def on_device(subject_data, template, neighbours, valid):
    blocks_here = template.shape[0]
    share = blocks_here // lax.axis_size("tm")
    subjects_all = subject_data.shape[0] * lax.axis_size("subj")
    offsets = neighbours - (lax.axis_index("slab") - 1) * blocks_here
    mask_all = valid.astype(jnp.float32)
    first = lax.axis_index("tm") * share
    my_offsets = lax.dynamic_slice_in_dim(offsets, first, share, 0)
    my_mask = lax.dynamic_slice_in_dim(mask_all, first, share, 0)
    full_time = gather_directly(subject_data, "tm", 3)
    extended = with_halo(full_time, (("slab", 1),), blocks_here)
    mine = lax.all_to_all(template, "tm", split_axis=0, concat_axis=2, tiled=True)
    col_norm = lax.rsqrt(square_sum(extended) + 1e-06)
    row_norm = lax.rsqrt(square_sum(mine) + 1e-06)

    def one_block(inputs):
        tmpl_block, scale_rows, slots, mask = inputs
        cross = slot_cross(tmpl_block, extended, slots)
        plan = balance(cross, scale_rows, jnp.take(col_norm, slots, axis=1), mask)
        return project(plan, extended, slots)

    moved = lax.map(one_block, (mine, row_norm, my_offsets, my_mask))
    averaged = subject_mean(moved, subjects_all)
    return exchange_in_pieces(averaged, "tm", 2, 2, 0)


def solution(mesh):
    placed = (
        P("subj", "slab", None, "tm"),
        P("slab", None, "tm"),
        P("slab", None),
        P("slab", None),
    )
    return jax.shard_map(
        on_device, mesh=mesh, in_specs=placed, out_specs=P("slab", None, "tm"), check_vma=False
    )
```

profile of v0, /device:TPU:2, one launch (start us, length us, event | category | flops | bytes accessed | tf_op | source)
XLA Modules:
  0.0 117.3 jit_solution(14926200425164752471)
XLA Ops:
  0.0 2.2 %broadcast_in_dim.73 = bf16[2,1,2,128,1024]{4,3,2,1,0:T(8,128)(2,1)} broadcast(bf16[2,128,1024]{2,1,0:T(8,128)(2,1)} %bitcast.117), dimensions={2,3,4} | broadcast | bytes 1572864 | tf_op jit(solution)/shard_map/broadcast_in_dim | solution.py:11
  2.2 3.6 %all-to-all-start = ((bf16[2,1,2,128,1024]{4,3,2,1,0:T(8,128)(2,1)}), bf16[2,1,2,128,1024]{4,3,2,1,0:T(8,128)(2,1)S(1)}, u32[]{:S(2)}, u32[]{:S(2)}) async-start(bf16[2,1,2,128,1024]{4,3,2,1,0:T(8,128)(2,1)} %broadcast_in_dim.73), calls=%async_computation | async-start | bytes 2097152 | tf_op jit(solution)/shard_map/all_to_all | solution.py:11
  5.8 15.3 %all-to-all-done = bf16[2,1,2,128,1024]{4,3,2,1,0:T(8,128)(2,1)S(1)} async-done(((bf16[2,1,2,128,1024]{4,3,2,1,0:T(8,128)(2,1)}), bf16[2,1,2,128,1024]{4,3,2,1,0:T(8,128)(2,1)S(1)}, u32[]{:S(2)}, u32[]{:S(2)}) %all-to-all-start) | async-done | bytes 1048608 | tf_op jit(solution)/shard_map/all_to_all | solution.py:11
  21.1 3.5 %all-to-all-start.1 = ((bf16[2,128,1024]{2,1,0:T(8,128)(2,1)}), bf16[2,128,1024]{2,1,0:T(8,128)(2,1)S(1)}, u32[]{:S(2)}, u32[]{:S(2)}) async-start(bf16[2,128,1024]{2,1,0:T(8,128)(2,1)} %param.5), calls=%async_computation.1 | async-start | bytes 1048576 | tf_op jit(solution)/shard_map/all_to_all | solution.py:119
  24.7 10.6 %collective-permute-start.1 = (bf16[1,2,128,2048]{3,2,1,0:T(8,128)(2,1)S(1)}, bf16[1,2,128,2048]{3,2,1,0:T(8,128)(2,1)}, u32[]{:S(2)}, u32[]{:S(2)}) collective-permute-start(bf16[1,2,128,2048]{3,2,1,0:T(8,128)(2,1)S(1)} %bitcast.108), channel_id=1, source_target_pairs={{4,0},{8,4},{12,8},{16,12},{20,16},{24,20},{28,24},{32,28},{36,32}... | collective-permute-start | bytes 3145736 | tf_op jit(solution)/shard_map/ppermute | solution.py:39
  35.3 1.9 %collective-permute-start = (bf16[1,2,128,2048]{3,2,1,0:T(8,128)(2,1)S(1)}, bf16[1,2,128,2048]{3,2,1,0:T(8,128)(2,1)}, u32[]{:S(2)}, u32[]{:S(2)}) collective-permute-start(bf16[1,2,128,2048]{3,2,1,0:T(8,128)(2,1)S(1)} %bitcast.109), channel_id=1, source_target_pairs={{0,4},{4,8},{8,12},{12,16},{16,20},{20,24},{24,28},{28,32},{32,36}... | collective-permute-start | bytes 3145736 | tf_op jit(solution)/shard_map/ppermute | solution.py:37
  39.9 16.6 %collective-permute-done.1 = bf16[1,2,128,2048]{3,2,1,0:T(8,128)(2,1)} collective-permute-done((bf16[1,2,128,2048]{3,2,1,0:T(8,128)(2,1)S(1)}, bf16[1,2,128,2048]{3,2,1,0:T(8,128)(2,1)}, u32[]{:S(2)}, u32[]{:S(2)}) %collective-permute-start.1) | collective-permute-done | bytes 1048608 | tf_op jit(solution)/shard_map/ppermute | solution.py:39
  56.5 8.4 %collective-permute-done = bf16[1,2,128,2048]{3,2,1,0:T(8,128)(2,1)} collective-permute-done((bf16[1,2,128,2048]{3,2,1,0:T(8,128)(2,1)S(1)}, bf16[1,2,128,2048]{3,2,1,0:T(8,128)(2,1)}, u32[]{:S(2)}, u32[]{:S(2)}) %collective-permute-start) | collective-permute-done | bytes 1048608 | tf_op jit(solution)/shard_map/ppermute | solution.py:37
  65.0 2.0 %fusion = f32[6,128]{1,0:T(8,128)S(1)} fusion(bf16[1,2,128,2048]{3,2,1,0:T(8,128)(2,1)} %collective-permute-done.1, bf16[1,2,128,2048]{3,2,1,0:T(8,128)(2,1)S(1)} %bitcast.110, bf16[1,2,128,2048]{3,2,1,0:T(8,128)(2,1)} %collective-permute-done), kind=kLoop, calls=%fused_computation.3 | loop fusion | flops 7863552 | bytes 3148800 | tf_op jit(solution)/shard_map/...t,...t->.../dot_general | solution.py:82
  67.5 2.5 %convolution_bitcast_fusion.3 = f32[128,6,128]{0,2,1:T(8,128)S(1)} fusion(bf16[128,2048,1]{1,0,2:T(8,128)(2,1)S(1)} %reshape.364, bf16[1,2,128,2048]{3,2,1,0:T(8,128)(2,1)} %collective-permute-done.1, bf16[1,2,128,2048]{3,2,1,0:T(8,128)(2,1)S(1)} %bitcast.111, bf16[1,2,128,2048]{3,2,1,0:T(8,128)(2,1)} %collective-permute-done), kind=kOutput, calls=%fused_computation.30 | convolution fusion | flops 405798912 | bytes 4063232 | tf_op jit(solution)/shard_map/while/body/eval_jaxpr/it,sejt->siej/dot_general | solution.py:86
  71.6 1.4 %multiply_reduce_fusion.5 = f32[27,128]{1,0:T(8,128)S(1)} fusion(f32[128]{0:T(128)S(1)} %broadcast_divide_fusion.2, f32[27]{0:T(128)S(1)} %get-tuple-element.20, f32[27,128]{1,0:T(8,128)S(1)} %broadcast_select_fusion, f32[128]{0:T(128)S(1)} %add_rsqrt_fusion.1, f32[27,128,128]{1,2,0:T(8,128)S(1)} %gather_fusion, pred[27]{0:T(512)(128)(4,1)S(1)} %get-tuple-element.21), kind=kLoop, calls=%fused_computation.27 | loop fusion | flops 3093120 | bytes 1798279 | tf_op jit(solution)/shard_map/while/body/eval_jaxpr/reduce_sum | solution.py:76
  73.1 1.3 %multiply_reduce_fusion.4 = f32[128]{0:T(128)S(1)} fusion(f32[27,128]{1,0:T(8,128)S(1)} %add_divide_fusion.2, f32[27]{0:T(128)S(1)} %get-tuple-element.20, f32[27,128]{1,0:T(8,128)S(1)} %broadcast_select_fusion, f32[128]{0:T(128)S(1)} %add_rsqrt_fusion.1, f32[27,128,128]{1,2,0:T(8,128)S(1)} %gather_fusion, pred[27]{0:T(512)(128)(4,1)S(1)} %get-tuple-element.21), kind=kLoop, calls=%fused_computation.26 | loop fusion | flops 3096448 | bytes 1798279 | tf_op jit(solution)/shard_map/while/body/eval_jaxpr/reduce_sum | solution.py:75
  74.4 1.4 %multiply_reduce_fusion.3 = f32[27,128]{1,0:T(8,128)S(1)} fusion(f32[128]{0:T(128)S(1)} %broadcast_divide_fusion.1, f32[27]{0:T(128)S(1)} %get-tuple-element.20, f32[27,128]{1,0:T(8,128)S(1)} %broadcast_select_fusion, f32[128]{0:T(128)S(1)} %add_rsqrt_fusion.1, f32[27,128,128]{1,2,0:T(8,128)S(1)} %gather_fusion, pred[27]{0:T(512)(128)(4,1)S(1)} %get-tuple-element.21), kind=kLoop, calls=%fused_computation.25 | loop fusion | flops 3093120 | bytes 1798279 | tf_op jit(solution)/shard_map/while/body/eval_jaxpr/reduce_sum | solution.py:76
  75.9 1.3 %multiply_reduce_fusion.2 = f32[128]{0:T(128)S(1)} fusion(f32[27,128]{1,0:T(8,128)S(1)} %add_divide_fusion.1, f32[27]{0:T(128)S(1)} %get-tuple-element.20, f32[27,128]{1,0:T(8,128)S(1)} %broadcast_select_fusion, f32[128]{0:T(128)S(1)} %add_rsqrt_fusion.1, f32[27,128,128]{1,2,0:T(8,128)S(1)} %gather_fusion, pred[27]{0:T(512)(128)(4,1)S(1)} %get-tuple-element.21), kind=kLoop, calls=%fused_computation.24 | loop fusion | flops 3096448 | bytes 1798279 | tf_op jit(solution)/shard_map/while/body/eval_jaxpr/reduce_sum | solution.py:75
  77.3 1.4 %multiply_reduce_fusion.1 = f32[27,128]{1,0:T(8,128)S(1)} fusion(f32[128]{0:T(128)S(1)} %broadcast_divide_fusion, f32[27]{0:T(128)S(1)} %get-tuple-element.20, f32[27,128]{1,0:T(8,128)S(1)} %broadcast_select_fusion, f32[128]{0:T(128)S(1)} %add_rsqrt_fusion.1, f32[27,128,128]{1,2,0:T(8,128)S(1)} %gather_fusion, pred[27]{0:T(512)(128)(4,1)S(1)} %get-tuple-element.21), kind=kLoop, calls=%fused_computation.23 | loop fusion | flops 3093120 | bytes 1798279 | tf_op jit(solution)/shard_map/while/body/eval_jaxpr/reduce_sum | solution.py:76
  78.7 1.3 %multiply_reduce_fusion = f32[128]{0:T(128)S(1)} fusion(f32[27,128]{1,0:T(8,128)S(1)} %add_divide_fusion, f32[27]{0:T(128)S(1)} %get-tuple-element.20, f32[27,128]{1,0:T(8,128)S(1)} %broadcast_select_fusion, f32[128]{0:T(128)S(1)} %add_rsqrt_fusion.1, f32[27,128,128]{1,2,0:T(8,128)S(1)} %gather_fusion, pred[27]{0:T(512)(128)(4,1)S(1)} %get-tuple-element.21), kind=kLoop, calls=%fused_computation.22 | loop fusion | flops 3096448 | bytes 1798279 | tf_op jit(solution)/shard_map/while/body/eval_jaxpr/reduce_sum | solution.py:78
  80.1 2.3 %fusion.14 = bf16[128,27,128]{0,2,1:T(8,128)(2,1)} fusion(f32[27,128,128]{1,2,0:T(8,128)S(1)} %gather_fusion, f32[128]{0:T(128)S(1)} %multiply_reduce_fusion, f32[27,128]{1,0:T(8,128)S(1)} %add_divide_fusion, f32[27]{0:T(128)S(1)} %get-tuple-element.20, f32[27,128]{1,0:T(8,128)S(1)} %broadcast_select_fusion, f32[128]{0:T(128)S(1)} %add_rsqrt_fusion.1, ...), kind=kLoop, calls=%fused_computation.28 | loop fusion | flops 3538944 | bytes 2683015 | tf_op jit(solution)/shard_map/while/body/eval_jaxpr/convert_element_type | solution.py:78
  82.4 1.9 %copy.23 = bf16[128,27,128]{2,1,0:T(8,128)(2,1)S(1)} copy(bf16[128,27,128]{0,2,1:T(8,128)(2,1)} %fusion.14) | data formatting | bytes 1769472 | tf_op jit(solution)/shard_map/while/body/eval_jaxpr/convert_element_type | solution.py:78
  84.6 2.3 %convolution_bitcast_fusion = f32[128,2048]{1,0:T(8,128)S(1)} fusion(bf16[128,6,128]{2,1,0:T(8,128)(2,1)S(1)} %get-tuple-element.36, bf16[1,2,128,2048]{3,2,1,0:T(8,128)(2,1)} %collective-permute-done.1, bf16[1,2,128,2048]{3,2,1,0:T(8,128)(2,1)S(1)} %bitcast.112, bf16[1,2,128,2048]{3,2,1,0:T(8,128)(2,1)} %collective-permute-done), kind=kOutput, calls=%fused_computation.5 | convolution fusion | flops 405798912 | bytes 4390912 | tf_op jit(solution)/shard_map/while/body/eval_jaxpr/siej,sejt->it/dot_general | solution.py:100
  86.9 2.3 %fusion.1 = f32[128,2048]{1,0:T(8,128)S(1)} fusion(f32[128,2048]{1,0:T(8,128)S(1)} %convolution_bitcast_fusion, bf16[128,6,128]{2,1,0:T(8,128)(2,1)S(1)} %get-tuple-element.34, bf16[1,2,128,2048]{3,2,1,0:T(8,128)(2,1)} %collective-permute-done.1, bf16[1,2,128,2048]{3,2,1,0:T(8,128)(2,1)S(1)} %bitcast.113, bf16[1,2,128,2048]{3,2,1,0:T(8,128)(2,1)} %collective-permute-done), kind=kOutput, calls=%fused_computation.7 | convolution fusion | flops 406061056 | bytes 5439488 | tf_op jit(solution)/shard_map/while/body/eval_jaxpr/siej,sejt->it/dot_general | solution.py:99
  89.4 5.4 %all_to_all.35 = f32[2,1,128,2048]{3,2,1,0:T(8,128)S(1)} all-to-all(f32[2,1,128,2048]{3,2,1,0:T(8,128)S(1)} %broadcast_in_dim.79), channel_id=1, replica_groups=mesh['slab'=64,'subj'=2,'tm'=2] {'subj'}, dimensions={0} | all-to-all | bytes 4194304 | tf_op jit(solution)/shard_map/all_to_all | solution.py:11
  96.5 3.9 %all-to-all-start.3 = ((bf16[2,1,64,1024]{3,2,1,0:T(8,128)(2,1)}), bf16[2,1,64,1024]{3,2,1,0:T(8,128)(2,1)S(1)}, u32[]{:S(2)}, u32[]{:S(2)}) async-start(bf16[2,1,64,1024]{3,2,1,0:T(8,128)(2,1)} %copy.27), calls=%async_computation.3 | async-start | bytes 524288 | tf_op jit(solution)/shard_map/all_to_all | solution.py:62
  100.6 6.8 %all-to-all-done.3 = bf16[2,1,64,1024]{3,2,1,0:T(8,128)(2,1)S(1)} async-done(((bf16[2,1,64,1024]{3,2,1,0:T(8,128)(2,1)}), bf16[2,1,64,1024]{3,2,1,0:T(8,128)(2,1)S(1)}, u32[]{:S(2)}, u32[]{:S(2)}) %all-to-all-start.3) | async-done | bytes 262176 | tf_op jit(solution)/shard_map/all_to_all | solution.py:62
  107.4 9.1 %all_to_all.36 = bf16[2,1,64,1024]{3,2,1,0:T(8,128)(2,1)S(1)} all-to-all(bf16[2,1,64,1024]{3,2,1,0:T(8,128)(2,1)S(1)} %copy.28), channel_id=1, replica_groups=mesh['slab'=64,'subj'=2,'tm'=2] {'tm'}, dimensions={0} | all-to-all | bytes 524288 | tf_op jit(solution)/shard_map/all_to_all | solution.py:62
  (39 shorter events, 7.6 us)
Async XLA Ops:
  2.2 18.9 %all-to-all-start = ((bf16[2,1,2,128,1024]{4,3,2,1,0:T(8,128)(2,1)}), bf16[2,1,2,128,1024]{4,3,2,1,0:T(8,128)(2,1)S(1)}, u32[]{:S(2)}, u32[]{:S(2)}) async-start(bf16[2,1,2,128,1024]{4,3,2,1,0:T(8,128)(2,1)} %broadcast_in_dim.73), calls=%async_computation | async-start | bytes 2097152 | tf_op jit(solution)/shard_map/all_to_all | solution.py:11
  5.7 31.5 %copy-start = (s32[2,27]{1,0:T(2,128)S(1)}, s32[2,27]{1,0:T(2,128)}, u32[]{:S(2)}) copy-start(s32[2,27]{1,0:T(2,128)} %param.6) | copy-start | bytes 652
  5.8 31.5 %copy-start.1 = (s32[2,27]{1,0:T(2,128)S(1)}, s32[2,27]{1,0:T(2,128)}, u32[]{:S(2)}) copy-start(s32[2,27]{1,0:T(2,128)} %param.7) | copy-start | bytes 652
  21.1 17.6 %all-to-all-start.1 = ((bf16[2,128,1024]{2,1,0:T(8,128)(2,1)}), bf16[2,128,1024]{2,1,0:T(8,128)(2,1)S(1)}, u32[]{:S(2)}, u32[]{:S(2)}) async-start(bf16[2,128,1024]{2,1,0:T(8,128)(2,1)} %param.5), calls=%async_computation.1 | async-start | bytes 1048576 | tf_op jit(solution)/shard_map/all_to_all | solution.py:119
  24.7 31.8 %collective-permute-start.1 = (bf16[1,2,128,2048]{3,2,1,0:T(8,128)(2,1)S(1)}, bf16[1,2,128,2048]{3,2,1,0:T(8,128)(2,1)}, u32[]{:S(2)}, u32[]{:S(2)}) collective-permute-start(bf16[1,2,128,2048]{3,2,1,0:T(8,128)(2,1)S(1)} %bitcast.108), channel_id=1, source_target_pairs={{4,0},{8,4},{12,8},{16,12},{20,16},{24,20},{28,24},{32,28},{36,32}... | collective-permute-start | bytes 3145736 | tf_op jit(solution)/shard_map/ppermute | solution.py:39
  35.3 29.6 %collective-permute-start = (bf16[1,2,128,2048]{3,2,1,0:T(8,128)(2,1)S(1)}, bf16[1,2,128,2048]{3,2,1,0:T(8,128)(2,1)}, u32[]{:S(2)}, u32[]{:S(2)}) collective-permute-start(bf16[1,2,128,2048]{3,2,1,0:T(8,128)(2,1)S(1)} %bitcast.109), channel_id=1, source_target_pairs={{0,4},{4,8},{8,12},{12,16},{16,20},{20,24},{24,28},{28,32},{32,36}... | collective-permute-start | bytes 3145736 | tf_op jit(solution)/shard_map/ppermute | solution.py:37
  96.5 10.9 %all-to-all-start.3 = ((bf16[2,1,64,1024]{3,2,1,0:T(8,128)(2,1)}), bf16[2,1,64,1024]{3,2,1,0:T(8,128)(2,1)S(1)}, u32[]{:S(2)}, u32[]{:S(2)}) async-start(bf16[2,1,64,1024]{3,2,1,0:T(8,128)(2,1)} %copy.27), calls=%async_computation.3 | async-start | bytes 524288 | tf_op jit(solution)/shard_map/all_to_all | solution.py:62
where the time goes:
time: 118 us; the launch traced here: 117 us
  waiting for transfers between devices  47.2 us (40%)
  starting transfers between devices  23.5 us (20%)
  other arithmetic  15.5 us (13%)
  blocking collectives  14.5 us (12%)
  local copies, waits for them, and re-layouts  8.28 us (7%)
  matrix products  7.33 us (6%)
    ppermute x1, waiting for transfers between devices, with_halo(): lax.ppermute(head, axis, [((i + 1) % count, i) for i in range(ends)])  16.6 us
    all_to_all x1, waiting for transfers between devices, from_everyone(): lax.all_to_all(jnp.broadcast_to(x[None], (size, *x.shape)), axis, 0, 0, t...  15.3 us
    ppermute x1, starting transfers between devices, with_halo(): lax.ppermute(head, axis, [((i + 1) % count, i) for i in range(ends)])  10.6 us
    all_to_all x1, blocking collectives, exchange_in_pieces(): lax.all_to_all(piece, axis, split_axis=0, concat_axis=0, tiled=True)  9.06 us
    ppermute x1, waiting for transfers between devices, with_halo(): lax.ppermute(tail, axis, [(i, (i + 1) % count) for i in range(ends)])  8.44 us
    all_to_all x1, waiting for transfers between devices, exchange_in_pieces(): lax.all_to_all(piece, axis, split_axis=0, concat_axis=0, tiled=True)  6.77 us
    all_to_all x1, blocking collectives, from_everyone(): lax.all_to_all(jnp.broadcast_to(x[None], (size, *x.shape)), axis, 0, 0, t...  5.42 us
    reduce_sum x3, other arithmetic, balance(): jnp.sum(kernel * row_weight, axis=1, keepdims=True) + filler  4.12 us
  transfers between devices with their start and end apart: 5, of which 4 were waited for; matrix products, arithmetic and copies ran while one was open for 2% of the time, Pallas kernels for 0%

commit v1 on v0

v1 whole, which is shorter than its diff:
```python
import jax
import jax.numpy as jnp
from jax import lax
from jax.experimental import pallas as pl
from jax.experimental.pallas import tpu as pltpu
from jax.sharding import PartitionSpec as P

MESH = pl.DeviceIdType.MESH
ITERS = 3
SCALE = 32760.0
TINY = 1e-6
PIECES = 4
OUT_PIECES = 4


def times_transposed(a, b):
    return lax.dot_general(a, b, (((1,), (1,)), ((), ())), preferred_element_type=jnp.float32)


def body(
    data_ref, tmpl_ref, near_ref, valid_ref, mine_ref, theirs_ref,
    ext, tmpl, part, code_out, code_in, norm_out, norm_in, kern, plan, moved,
    local_sem, slab_send, slab_recv, code_send, code_recv, norm_send, norm_recv, subj_send, subj_recv, mine_sem,
):
    slab, slabs = lax.axis_index("slab"), lax.axis_size("slab")
    subj, half = lax.axis_index("subj"), lax.axis_index("tm")
    rows, times = data_ref.shape
    width = 128
    blocks = rows // width
    piece = rows // PIECES
    tiles = blocks + PIECES
    has_prev, has_next = slab > 0, slab < slabs - 1

    copies = [
        pltpu.make_async_copy(tmpl_ref, tmpl, local_sem.at[0]),
        pltpu.make_async_copy(data_ref, ext.at[pl.ds(0, rows)], local_sem.at[1]),
    ]
    for copy in copies:
        copy.start()

    barrier = pltpu.get_barrier_semaphore()

    def greet(where):
        pl.semaphore_signal(barrier, inc=1, device_id=where, device_id_type=MESH)

    greet({"subj": 1 - subj})
    greet({"tm": 1 - half})

    @pl.when(has_prev)
    def _():
        greet({"slab": slab - 1})

    @pl.when(has_next)
    def _():
        greet({"slab": slab + 1})

    @pl.when(has_prev & has_next)
    def _():
        pl.semaphore_wait(barrier, 4)

    @pl.when(jnp.logical_not(has_prev & has_next))
    def _():
        pl.semaphore_wait(barrier, 3)

    def slab_copy(q, up):
        place = blocks * width + q * 2 * piece + (0 if up else piece)
        k = q + (0 if up else PIECES)
        return pltpu.make_async_remote_copy(
            src_ref=data_ref.at[pl.ds(q * piece, piece)],
            dst_ref=ext.at[pl.ds(place, piece)],
            send_sem=slab_send.at[k],
            recv_sem=slab_recv.at[k],
            device_id={"slab": slab + 1 if up else slab - 1},
            device_id_type=MESH,
        )

    for q in range(PIECES):

        @pl.when(has_next)
        def _():
            slab_copy(q, True).start()

        @pl.when(has_prev)
        def _():
            slab_copy(q, False).start()

    @pl.when(jnp.logical_not(has_prev))
    def _():
        for q in range(PIECES):
            ext[pl.ds(blocks * width + q * 2 * piece, piece), :] = jnp.zeros((piece, times), ext.dtype)

    @pl.when(jnp.logical_not(has_next))
    def _():
        for q in range(PIECES):
            ext[pl.ds(blocks * width + q * 2 * piece + piece, piece), :] = jnp.zeros((piece, times), ext.dtype)

    seen = near_ref[...] - (slab - 1) * blocks
    used = valid_ref[...].astype(jnp.float32)
    count = [
        jnp.sum(jnp.where(seen == e, used, 0.0), axis=1, keepdims=True) for e in range(3 * blocks)
    ]
    goal = 1.0 / (width * jnp.sum(used, axis=1, keepdims=True))
    lane = lax.broadcasted_iota(jnp.int32, (1, width), 1)

    def counts(b, tile):
        if tile < blocks:
            return jnp.broadcast_to(count[blocks + tile][b : b + 1], (1, width))
        owner = (tile - blocks) * piece // width
        return jnp.where(lane < piece, count[owner][b : b + 1], count[2 * blocks + owner][b : b + 1])

    eye = lax.broadcasted_iota(jnp.int32, (width, width), 0) == lax.broadcasted_iota(
        jnp.int32, (width, width), 1
    )

    def diagonal(gram, axis):
        return jnp.sum(jnp.where(eye, gram, 0.0), axis=axis, keepdims=True)

    copies[0].wait()
    grams = [
        times_transposed(tmpl[pl.ds(b * width, width), :], tmpl[pl.ds(b * width, width), :])
        for b in range(blocks)
    ]
    row_sq = [diagonal(gram, 1) for gram in grams]
    row_unit = [lax.rsqrt(sq + TINY) * SCALE for sq in row_sq]

    def code_copy(tile):
        return pltpu.make_async_remote_copy(
            src_ref=code_out.at[tile], dst_ref=code_in.at[tile],
            send_sem=code_send.at[tile], recv_sem=code_recv.at[tile],
            device_id={"tm": 1 - half}, device_id_type=MESH,
        )

    def norm_copy(tile):
        return pltpu.make_async_remote_copy(
            src_ref=norm_out.at[tile], dst_ref=norm_in.at[tile],
            send_sem=norm_send.at[tile], recv_sem=norm_recv.at[tile],
            device_id={"tm": 1 - half}, device_id_type=MESH,
        )

    def first_pass(tile):
        data = ext[pl.ds(tile * width, width), :]
        col_sq = diagonal(times_transposed(data, data), 0)
        norm_out[tile] = jnp.concatenate(
            [col_sq] + [diagonal(gram, 0) for gram in grams] + [jnp.zeros((8 - 1 - blocks, width), jnp.float32)], axis=0
        )
        norm_copy(tile).start()
        col_unit = lax.rsqrt(col_sq + TINY)
        for b in range(blocks):
            at = pl.ds(b * width, width)
            cross = times_transposed(tmpl[at, :], data)
            part[tile, at, :] = cross
            code_out[tile, at, :] = jnp.round(cross * row_unit[b] * col_unit).astype(jnp.int32).astype(jnp.int16)
        code_copy(tile).start()

    scales = {}

    def second_pass(tile):
        norm_copy(tile).wait_recv()
        there = norm_in[tile]
        if tile == 0:
            for b in range(blocks):
                other = jnp.sum(jnp.where(eye, there[1 + b : 2 + b], 0.0), axis=1, keepdims=True)
                row_scale = lax.rsqrt(row_sq[b] + other + 1e-6)
                scales[b] = (row_scale, row_scale * ((other + TINY) * lax.rsqrt(other + TINY)))
        col_sq = norm_out[tile][0:1]
        other = there[0:1]
        col_scale = lax.rsqrt(col_sq + other + 1e-6) * (1.0 / 0.03)
        col_other = col_scale * ((other + TINY) * lax.rsqrt(other + TINY)) * (1.0 / SCALE)
        code_copy(tile).wait_recv()
        for b in range(blocks):
            at = pl.ds(b * width, width)
            logits = part[tile, at, :] * (scales[b][0] * col_scale)
            logits += code_in[tile, at, :].astype(jnp.int32).astype(jnp.float32) * (scales[b][1] * col_other)
            kern[tile, at, :] = jnp.exp(logits)

    def arrived(q):
        @pl.when(has_prev)
        def _():
            slab_copy(q, True).wait_recv()

        @pl.when(has_next)
        def _():
            slab_copy(q, False).wait_recv()

    copies[1].wait()
    for tile in range(blocks):
        first_pass(tile)
    behind = 0
    for q in range(PIECES):
        arrived(q)
        first_pass(blocks + q)
        while behind < blocks + q:
            second_pass(behind)
            behind += 1
    while behind < tiles:
        second_pass(behind)
        behind += 1

    for b in range(blocks):
        at = pl.ds(b * width, width)
        number = [counts(b, tile) for tile in range(tiles)]
        weight = number
        for _ in range(ITERS):
            total = sum(kern[tile, at, :] * weight[tile] for tile in range(tiles))
            row_weight = (1.0 / width) / jnp.sum(total, axis=1, keepdims=True)
            weight = [
                number[tile] * goal[b : b + 1] / jnp.sum(kern[tile, at, :] * row_weight, axis=0, keepdims=True)
                for tile in range(tiles)
            ]
        total = sum(kern[tile, at, :] * weight[tile] for tile in range(tiles))
        share = 0.5 / jnp.sum(total, axis=1, keepdims=True)
        for tile in range(tiles):
            plan[at, pl.ds(tile * width, width)] = (kern[tile, at, :] * weight[tile] * share).astype(plan.dtype)

    wide = times // OUT_PIECES
    moves = []
    for c in range(OUT_PIECES):
        at = (slice(None), pl.ds(c * wide, wide))
        moved[at] = jnp.dot(plan[...], ext[at], preferred_element_type=jnp.float32).astype(moved.dtype)
        moves.append(
            pltpu.make_async_remote_copy(
                src_ref=moved.at[at], dst_ref=theirs_ref.at[at],
                send_sem=subj_send.at[c], recv_sem=subj_recv.at[c],
                device_id={"subj": 1 - subj}, device_id_type=MESH,
            )
        )
        moves.append(pltpu.make_async_copy(moved.at[at], mine_ref.at[at], mine_sem.at[c]))
        for move in moves[-2:]:
            move.start()

    for tile in range(tiles):
        norm_copy(tile).wait_send()
        code_copy(tile).wait_send()
    for q in range(PIECES):

        @pl.when(has_next)
        def _():
            slab_copy(q, True).wait_send()

        @pl.when(has_prev)
        def _():
            slab_copy(q, False).wait_send()

    for move in moves:
        move.wait()


def on_device(subject_data, template, neighbours, valid):
    _, blocks, width, times = subject_data.shape
    rows = blocks * width
    tiles = blocks + PIECES
    dma = pltpu.SemaphoreType.DMA
    anywhere = pl.BlockSpec(memory_space=pl.ANY)
    vmem = pl.BlockSpec(memory_space=pltpu.VMEM)
    mine, theirs = pl.pallas_call(
        body,
        out_shape=[jax.ShapeDtypeStruct((rows, times), jnp.bfloat16)] * 2,
        in_specs=[anywhere, anywhere, vmem, vmem],
        out_specs=[anywhere, anywhere],
        scratch_shapes=[
            pltpu.VMEM((tiles * width, times), jnp.bfloat16),
            pltpu.VMEM((rows, times), jnp.bfloat16),
            pltpu.VMEM((tiles, rows, width), jnp.float32),
            pltpu.VMEM((tiles, rows, width), jnp.int16),
            pltpu.VMEM((tiles, rows, width), jnp.int16),
            pltpu.VMEM((tiles, 8, width), jnp.float32),
            pltpu.VMEM((tiles, 8, width), jnp.float32),
            pltpu.VMEM((tiles, rows, width), jnp.float32),
            pltpu.VMEM((rows, tiles * width), jnp.bfloat16),
            pltpu.VMEM((rows, times), jnp.bfloat16),
            dma((2,)),
            dma((2 * PIECES,)), dma((2 * PIECES,)),
            dma((tiles,)), dma((tiles,)),
            dma((tiles,)), dma((tiles,)),
            dma((OUT_PIECES,)), dma((OUT_PIECES,)), dma((OUT_PIECES,)),
        ],
        compiler_params=pltpu.CompilerParams(
            collective_id=0, has_side_effects=True, vmem_limit_bytes=32 * 2**20
        ),
    )(subject_data.reshape(rows, times), template.reshape(rows, times), neighbours, valid)
    total = mine.astype(jnp.float32) + theirs.astype(jnp.float32)
    return total.astype(jnp.bfloat16).reshape(template.shape)


def solution(mesh):
    placed = (
        P("subj", "slab", None, "tm"),
        P("slab", None, "tm"),
        P("slab", None),
        P("slab", None),
    )
    return jax.shard_map(
        on_device, mesh=mesh, in_specs=placed, out_specs=P("slab", None, "tm"), check_vma=False
    )
```

time: 118 us -> 41.4 us (0.35)
  the two profiles are of different devices: /device:TPU:2 before, /device:TPU:25 now
where the time goes in v1:
time: 41.4 us; the launch traced here: 41.3 us
  Pallas kernels  37.5 us (91%)
  local copies, waits for them, and re-layouts  2.78 us (7%)
  other arithmetic  0.99 us (2%)
    pallas_call x1, Pallas kernels, on_device(): pl.pallas_call(body, out_shape=[jax.ShapeDtypeStruct((rows, times), jnp.b...  37.5 us
    unnamed x8, local copies, waits for them, and re-layouts  2.78 us
    convert_element_type x1, other arithmetic, on_device(): return total.astype(jnp.bfloat16).reshape(template.shape)  0.99 us

profile of v1, /device:TPU:25, one launch (start us, length us, event | category | flops | bytes accessed | tf_op | source)
XLA Modules:
  0.0 41.3 jit_solution(9493839902959657027)
XLA Ops:
  0.0 0.0 copy-start.3
  0.0 0.0 copy-start.2
  0.0 0.7 %copy-done.3 = s32[2,27]{1,0:T(2,128)S(1)} copy-done((s32[2,27]{1,0:T(2,128)S(1)}, s32[2,27]{1,0:T(2,128)}, u32[]{:S(2)}) %copy-start.3) | copy-done | bytes 240
  0.7 0.0 copy-done.2
  0.7 0.0 copy-start
  0.7 1.0 %copy-done = bf16[1,2,128,1024]{3,2,1,0:T(8,128)(2,1)S(1)} copy-done((bf16[1,2,128,1024]{3,2,1,0:T(8,128)(2,1)S(1)}, bf16[1,2,128,1024]{3,2,1,0:T(8,128)(2,1)}, u32[]{:S(2)}) %copy-start) | copy-done | bytes 524312
  1.7 0.0 copy-start.1
  1.7 1.0 %copy-done.1 = bf16[2,128,1024]{2,1,0:T(8,128)(2,1)S(1)} copy-done((bf16[2,128,1024]{2,1,0:T(8,128)(2,1)S(1)}, bf16[2,128,1024]{2,1,0:T(8,128)(2,1)}, u32[]{:S(2)}) %copy-start.1) | copy-done | bytes 524312
  2.8 37.5 %shard_map.46 = (bf16[256,1024]{1,0:T(8,128)(2,1)S(1)}, bf16[256,1024]{1,0:T(8,128)(2,1)S(1)}) custom-call(bf16[256,1024]{1,0:T(8,128)(2,1)S(1)} %bitcast.3, bf16[256,1024]{1,0:T(8,128)(2,1)S(1)} %bitcast.4, s32[2,27]{1,0:T(2,128)S(1)} %copy-done.2, s32[2,27]{1,0:T(2,128)S(1)} %copy-done.3), custom_call_target="tpu_custom_call" | custom-call | tf_op jit(solution)/shard_map/pallas_call | solution.py:255
  40.3 1.0 %add_convert_fusion = bf16[256,1024]{1,0:T(8,128)(2,1)} fusion(bf16[256,1024]{1,0:T(8,128)(2,1)S(1)} %get-tuple-element.8, bf16[256,1024]{1,0:T(8,128)(2,1)S(1)} %get-tuple-element.7), kind=kLoop, calls=%fused_computation | loop fusion | flops 1048576 | bytes 1572864 | tf_op jit(solution)/shard_map/convert_element_type | solution.py:282
Async XLA Ops:
  0.0 0.7 %copy-start.3 = (s32[2,27]{1,0:T(2,128)S(1)}, s32[2,27]{1,0:T(2,128)}, u32[]{:S(2)}) copy-start(s32[2,27]{1,0:T(2,128)} %valid_ref.1) | copy-start | bytes 652
  0.0 0.7 %copy-start.2 = (s32[2,27]{1,0:T(2,128)S(1)}, s32[2,27]{1,0:T(2,128)}, u32[]{:S(2)}) copy-start(s32[2,27]{1,0:T(2,128)} %near_ref.1) | copy-start | bytes 652
  0.7 1.0 %copy-start = (bf16[1,2,128,1024]{3,2,1,0:T(8,128)(2,1)S(1)}, bf16[1,2,128,1024]{3,2,1,0:T(8,128)(2,1)}, u32[]{:S(2)}) copy-start(bf16[1,2,128,1024]{3,2,1,0:T(8,128)(2,1)} %param.4) | copy-start | bytes 1572868
  1.7 1.0 %copy-start.1 = (bf16[2,128,1024]{2,1,0:T(8,128)(2,1)S(1)}, bf16[2,128,1024]{2,1,0:T(8,128)(2,1)}, u32[]{:S(2)}) copy-start(bf16[2,128,1024]{2,1,0:T(8,128)(2,1)} %param.5) | copy-start | bytes 1572868

commit v2 on v1

--- a/solution.py
+++ b/solution.py
@@ -10,6 +10,7 @@
 SCALE = 32760.0
 TINY = 1e-6
 PIECES = 4
+PASSED = (2, 3)
 OUT_PIECES = 4
 
 
@@ -19,8 +20,8 @@
 
 def body(
     data_ref, tmpl_ref, near_ref, valid_ref, mine_ref, theirs_ref,
-    ext, tmpl, part, code_out, code_in, norm_out, norm_in, kern, plan, moved,
-    local_sem, slab_send, slab_recv, code_send, code_recv, norm_send, norm_recv, subj_send, subj_recv, mine_sem,
+    ext, tmpl, near, valid, relayed, part, code_out, code_in, norm_out, norm_in, kern, plan,
+    local_sem, slab_send, slab_recv, pass_send, pass_recv, code_send, code_recv, norm_send, norm_recv, subj_send, subj_recv,
 ):
     slab, slabs = lax.axis_index("slab"), lax.axis_size("slab")
     subj, half = lax.axis_index("subj"), lax.axis_index("tm")
@@ -29,11 +30,15 @@
     blocks = rows // width
     piece = rows // PIECES
     tiles = blocks + PIECES
-    has_prev, has_next = slab > 0, slab < slabs - 1
+    last, low, high = slabs - 1, slabs // 2 - 1, slabs // 2
+    has_prev, has_next = slab > 0, slab < last
+    at_edge, at_middle = (slab == 0) | (slab == last), (slab == low) | (slab == high)
 
     copies = [
         pltpu.make_async_copy(tmpl_ref, tmpl, local_sem.at[0]),
         pltpu.make_async_copy(data_ref, ext.at[pl.ds(0, rows)], local_sem.at[1]),
+        pltpu.make_async_copy(near_ref, near, local_sem.at[2]),
+        pltpu.make_async_copy(valid_ref, valid, local_sem.at[3]),
     ]
     for copy in copies:
         copy.start()
@@ -54,35 +59,85 @@
     def _():
         greet({"slab": slab + 1})
 
-    @pl.when(has_prev & has_next)
+    @pl.when(at_edge)
+    def _():
+        greet({"slab": low})
+        greet({"slab": high})
+        pl.semaphore_wait(barrier, 5)
+
+    @pl.when(at_middle)
+    def _():
+        greet({"slab": 0})
+        greet({"slab": last})
+        pl.semaphore_wait(barrier, 6)
+
+    @pl.when(jnp.logical_not(at_edge | at_middle))
     def _():
         pl.semaphore_wait(barrier, 4)
 
-    @pl.when(jnp.logical_not(has_prev & has_next))
-    def _():
-        pl.semaphore_wait(barrier, 3)
+    def slab_place(q, up):
+        return ext.at[pl.ds(blocks * width + q * 2 * piece + (0 if up else piece), piece)]
 
     def slab_copy(q, up):
-        place = blocks * width + q * 2 * piece + (0 if up else piece)
         k = q + (0 if up else PIECES)
         return pltpu.make_async_remote_copy(
             src_ref=data_ref.at[pl.ds(q * piece, piece)],
-            dst_ref=ext.at[pl.ds(place, piece)],
+            dst_ref=slab_place(q, up),
             send_sem=slab_send.at[k],
             recv_sem=slab_recv.at[k],
             device_id={"slab": slab + 1 if up else slab - 1},
             device_id_type=MESH,
         )
 
+    def pass_copy(q, up):
+        k = 0 if up else 1
+        return pltpu.make_async_remote_copy(
+            src_ref=data_ref.at[pl.ds(q * piece, piece)],
+            dst_ref=relayed.at[k],
+            send_sem=slab_send.at[q + (0 if up else PIECES)],
+            recv_sem=pass_recv.at[k],
+            device_id={"slab": 0 if q == PASSED[0] else last},
+            device_id_type=MESH,
+        )
+
+    for q in PASSED:
+        for up, here in ((True, low), (False, high)):
+
+            @pl.when(slab == here)
+            def _():
+                pass_copy(q, up).start()
+
     for q in range(PIECES):
 
-        @pl.when(has_next)
+        @pl.when(has_next & (slab != low) if q in PASSED else has_next)
         def _():
             slab_copy(q, True).start()
 
-        @pl.when(has_prev)
+        @pl.when(has_prev & (slab != high) if q in PASSED else has_prev)
         def _():
             slab_copy(q, False).start()
+
+    def onward(q, up):
+        return pltpu.make_async_remote_copy(
+            src_ref=relayed.at[0 if up else 1],
+            dst_ref=slab_place(q, up),
+            send_sem=pass_send.at[0 if up else 1],
+            recv_sem=slab_recv.at[q + (0 if up else PIECES)],
+            device_id={"slab": high if up else low},
+            device_id_type=MESH,
+        )
+
+    def pass_on(act):
+        for q, here in zip(PASSED, (0, last)):
+
+            @pl.when(slab == here)
+            def _():
+                for up in (True, False):
+                    act(q, up)
+
+    def pass_start(q, up):
+        pass_copy(q, up).wait_recv()
+        onward(q, up).start()
 
     @pl.when(jnp.logical_not(has_prev))
     def _():
@@ -94,8 +149,10 @@
         for q in range(PIECES):
             ext[pl.ds(blocks * width + q * 2 * piece + piece, piece), :] = jnp.zeros((piece, times), ext.dtype)
 
-    seen = near_ref[...] - (slab - 1) * blocks
-    used = valid_ref[...].astype(jnp.float32)
+    copies[2].wait()
+    copies[3].wait()
+    seen = near[...] - (slab - 1) * blocks
+    used = valid[...].astype(jnp.float32)
     count = [
         jnp.sum(jnp.where(seen == e, used, 0.0), axis=1, keepdims=True) for e in range(3 * blocks)
     ]
@@ -189,6 +246,8 @@
     for q in range(PIECES):
         arrived(q)
         first_pass(blocks + q)
+        if q == 0:
+            pass_on(pass_start)
         while behind < blocks + q:
             second_pass(behind)
             behind += 1
@@ -216,18 +275,17 @@
     moves = []
     for c in range(OUT_PIECES):
         at = (slice(None), pl.ds(c * wide, wide))
-        moved[at] = jnp.dot(plan[...], ext[at], preferred_element_type=jnp.float32).astype(moved.dtype)
+        mine_ref[at] = jnp.dot(plan[...], ext[at], preferred_element_type=jnp.float32).astype(mine_ref.dtype)
         moves.append(
             pltpu.make_async_remote_copy(
-                src_ref=moved.at[at], dst_ref=theirs_ref.at[at],
+                src_ref=mine_ref.at[at], dst_ref=theirs_ref.at[at],
                 send_sem=subj_send.at[c], recv_sem=subj_recv.at[c],
                 device_id={"subj": 1 - subj}, device_id_type=MESH,
             )
         )
-        moves.append(pltpu.make_async_copy(moved.at[at], mine_ref.at[at], mine_sem.at[c]))
-        for move in moves[-2:]:
-            move.start()
-
+        moves[-1].start()
+
+    pass_on(lambda q, up: onward(q, up).wait_send())
     for tile in range(tiles):
         norm_copy(tile).wait_send()
         code_copy(tile).wait_send()
@@ -250,16 +308,19 @@
     rows = blocks * width
     tiles = blocks + PIECES
     dma = pltpu.SemaphoreType.DMA
-    anywhere = pl.BlockSpec(memory_space=pl.ANY)
+    hbm = pl.BlockSpec(memory_space=pltpu.HBM)
     vmem = pl.BlockSpec(memory_space=pltpu.VMEM)
     mine, theirs = pl.pallas_call(
         body,
         out_shape=[jax.ShapeDtypeStruct((rows, times), jnp.bfloat16)] * 2,
-        in_specs=[anywhere, anywhere, vmem, vmem],
-        out_specs=[anywhere, anywhere],
+        in_specs=[hbm] * 4,
+        out_specs=[vmem] * 2,
         scratch_shapes=[
             pltpu.VMEM((tiles * width, times), jnp.bfloat16),
             pltpu.VMEM((rows, times), jnp.bfloat16),
+            pltpu.VMEM(neighbours.shape, neighbours.dtype),
+            pltpu.VMEM(valid.shape, valid.dtype),
+            pltpu.VMEM((2, rows // PIECES, times), jnp.bfloat16),
             pltpu.VMEM((tiles, rows, width), jnp.float32),
             pltpu.VMEM((tiles, rows, width), jnp.int16),
             pltpu.VMEM((tiles, rows, width), jnp.int16),
@@ -267,17 +328,17 @@
             pltpu.VMEM((tiles, 8, width), jnp.float32),
             pltpu.VMEM((tiles, rows, width), jnp.float32),
             pltpu.VMEM((rows, tiles * width), jnp.bfloat16),
-            pltpu.VMEM((rows, times), jnp.bfloat16),
-            dma((2,)),
+            dma((4,)),
             dma((2 * PIECES,)), dma((2 * PIECES,)),
+            dma((2,)), dma((2,)),
             dma((tiles,)), dma((tiles,)),
             dma((tiles,)), dma((tiles,)),
-            dma((OUT_PIECES,)), dma((OUT_PIECES,)), dma((OUT_PIECES,)),
+            dma((OUT_PIECES,)), dma((OUT_PIECES,)),
         ],
         compiler_params=pltpu.CompilerParams(
             collective_id=0, has_side_effects=True, vmem_limit_bytes=32 * 2**20
         ),
-    )(subject_data.reshape(rows, times), template.reshape(rows, times), neighbours, valid)
+    )(*[pltpu.with_memory_space_constraint(x, pltpu.HBM) for x in (subject_data.reshape(rows, times), template.reshape(rows, times), neighbours, valid)])
     total = mine.astype(jnp.float32) + theirs.astype(jnp.float32)
     return total.astype(jnp.bfloat16).reshape(template.shape)
 

time: 41.4 us -> 37.3 us (0.901)
  the two profiles are of different devices: /device:TPU:25 before, /device:TPU:3 now
where the time goes in v2:
time: 37.3 us; the launch traced here: 37.2 us
  Pallas kernels  36.2 us (97%)
  other arithmetic  0.99 us (3%)
    pallas_call x1, Pallas kernels, on_device(): pl.pallas_call(body, out_shape=[jax.ShapeDtypeStruct((rows, times), jnp.b...  36.2 us
    convert_element_type x1, other arithmetic, on_device(): return total.astype(jnp.bfloat16).reshape(template.shape)  0.99 us

profile of v2, /device:TPU:3, one launch (start us, length us, event | category | flops | bytes accessed | tf_op | source)
XLA Modules:
  0.0 37.2 jit_solution(13456541866417784063)
XLA Ops:
  0.0 36.2 %shard_map.46 = (bf16[256,1024]{1,0:T(8,128)(2,1)S(1)}, bf16[256,1024]{1,0:T(8,128)(2,1)S(1)}) custom-call(bf16[256,1024]{1,0:T(8,128)(2,1)} %bitcast.3, bf16[256,1024]{1,0:T(8,128)(2,1)} %bitcast.4, s32[2,27]{1,0:T(2,128)} %near_ref.1, s32[2,27]{1,0:T(2,128)} %valid_ref.1), custom_call_target="tpu_custom_call" | custom-call | tf_op jit(solution)/shard_map/pallas_call | solution.py:313
  36.2 1.0 %add_convert_fusion = bf16[256,1024]{1,0:T(8,128)(2,1)} fusion(bf16[256,1024]{1,0:T(8,128)(2,1)S(1)} %get-tuple-element.8, bf16[256,1024]{1,0:T(8,128)(2,1)S(1)} %get-tuple-element.7), kind=kLoop, calls=%fused_computation | loop fusion | flops 1048576 | bytes 1572864 | tf_op jit(solution)/shard_map/convert_element_type | solution.py:343

commit v3 on v1

--- a/solution.py
+++ b/solution.py
@@ -10,6 +10,8 @@
 SCALE = 32760.0
 TINY = 1e-6
 PIECES = 4
+RUN = 8
+DETOUR = (0, 1)
 OUT_PIECES = 4
 
 
@@ -19,8 +21,8 @@
 
 def body(
     data_ref, tmpl_ref, near_ref, valid_ref, mine_ref, theirs_ref,
-    ext, tmpl, part, code_out, code_in, norm_out, norm_in, kern, plan, moved,
-    local_sem, slab_send, slab_recv, code_send, code_recv, norm_send, norm_recv, subj_send, subj_recv, mine_sem,
+    ext, tmpl, near, valid, passing, part, code_out, code_in, norm_out, norm_in, kern, plan,
+    local_sem, slab_send, slab_recv, pass_send, pass_recv, code_send, code_recv, norm_send, norm_recv, subj_send, subj_recv,
 ):
     slab, slabs = lax.axis_index("slab"), lax.axis_size("slab")
     subj, half = lax.axis_index("subj"), lax.axis_index("tm")
@@ -30,10 +32,14 @@
     piece = rows // PIECES
     tiles = blocks + PIECES
     has_prev, has_next = slab > 0, slab < slabs - 1
+    shared = (slabs // 2 - RUN, slabs // 2 + RUN - 1)
+    byway = (shared[0] - RUN, shared[1] + RUN)
 
     copies = [
         pltpu.make_async_copy(tmpl_ref, tmpl, local_sem.at[0]),
         pltpu.make_async_copy(data_ref, ext.at[pl.ds(0, rows)], local_sem.at[1]),
+        pltpu.make_async_copy(near_ref, near, local_sem.at[2]),
+        pltpu.make_async_copy(valid_ref, valid, local_sem.at[3]),
     ]
     for copy in copies:
         copy.start()
@@ -54,20 +60,39 @@
     def _():
         greet({"slab": slab + 1})
 
-    @pl.when(has_prev & has_next)
+    for crowded, way in zip(shared, byway):
+
+        @pl.when(slab == crowded)
+        def _():
+            greet({"slab": way, "tm": 1 - half})
+
+        @pl.when(slab == way)
+        def _():
+            greet({"slab": crowded})
+
+    is_shared = (slab == shared[0]) | (slab == shared[1])
+    is_byway = (slab == byway[0]) | (slab == byway[1])
+
+    @pl.when(has_prev & has_next & jnp.logical_not(is_shared | is_byway))
     def _():
         pl.semaphore_wait(barrier, 4)
 
+    @pl.when(is_shared | is_byway)
+    def _():
+        pl.semaphore_wait(barrier, 5)
+
     @pl.when(jnp.logical_not(has_prev & has_next))
     def _():
         pl.semaphore_wait(barrier, 3)
 
+    def slab_place(q, up):
+        return ext.at[pl.ds(blocks * width + q * 2 * piece + (0 if up else piece), piece)]
+
     def slab_copy(q, up):
-        place = blocks * width + q * 2 * piece + (0 if up else piece)
         k = q + (0 if up else PIECES)
         return pltpu.make_async_remote_copy(
             src_ref=data_ref.at[pl.ds(q * piece, piece)],
-            dst_ref=ext.at[pl.ds(place, piece)],
+            dst_ref=slab_place(q, up),
             send_sem=slab_send.at[k],
             recv_sem=slab_recv.at[k],
             device_id={"slab": slab + 1 if up else slab - 1},
@@ -94,8 +119,10 @@
         for q in range(PIECES):
             ext[pl.ds(blocks * width + q * 2 * piece + piece, piece), :] = jnp.zeros((piece, times), ext.dtype)
 
-    seen = near_ref[...] - (slab - 1) * blocks
-    used = valid_ref[...].astype(jnp.float32)
+    copies[2].wait()
+    copies[3].wait()
+    seen = near[...] - (slab - 1) * blocks
+    used = valid[...].astype(jnp.float32)
     count = [
         jnp.sum(jnp.where(seen == e, used, 0.0), axis=1, keepdims=True) for e in range(3 * blocks)
     ]
@@ -130,6 +157,44 @@
             device_id={"tm": 1 - half}, device_id_type=MESH,
         )
 
+    def detour_copy(tile, way):
+        return pltpu.make_async_remote_copy(
+            src_ref=code_out.at[tile], dst_ref=passing.at[tile],
+            send_sem=code_send.at[tile], recv_sem=pass_recv.at[tile],
+            device_id={"slab": way}, device_id_type=MESH,
+        )
+
+    def onward_copy(tile, crowded):
+        return pltpu.make_async_remote_copy(
+            src_ref=passing.at[tile], dst_ref=code_in.at[tile],
+            send_sem=pass_send.at[tile], recv_sem=code_recv.at[tile],
+            device_id={"slab": crowded, "tm": 1 - half}, device_id_type=MESH,
+        )
+
+    def send_code(tile):
+        if tile not in DETOUR:
+            code_copy(tile).start()
+            return
+
+        @pl.when(jnp.logical_not(is_shared))
+        def _():
+            code_copy(tile).start()
+
+        for crowded, way in zip(shared, byway):
+
+            @pl.when(slab == crowded)
+            def _():
+                detour_copy(tile, way).start()
+
+    def pass_on():
+        for crowded, way in zip(shared, byway):
+
+            @pl.when(slab == way)
+            def _():
+                for tile in DETOUR:
+                    detour_copy(tile, way).wait_recv()
+                    onward_copy(tile, crowded).start()
+
     def norm_copy(tile):
         return pltpu.make_async_remote_copy(
             src_ref=norm_out.at[tile], dst_ref=norm_in.at[tile],
@@ -150,7 +215,7 @@
             cross = times_transposed(tmpl[at, :], data)
             part[tile, at, :] = cross
             code_out[tile, at, :] = jnp.round(cross * row_unit[b] * col_unit).astype(jnp.int32).astype(jnp.int16)
-        code_copy(tile).start()
+        send_code(tile)
 
     scales = {}
 
@@ -185,6 +250,7 @@
     copies[1].wait()
     for tile in range(blocks):
         first_pass(tile)
+    pass_on()
     behind = 0
     for q in range(PIECES):
         arrived(q)
@@ -216,17 +282,20 @@
     moves = []
     for c in range(OUT_PIECES):
         at = (slice(None), pl.ds(c * wide, wide))
-        moved[at] = jnp.dot(plan[...], ext[at], preferred_element_type=jnp.float32).astype(moved.dtype)
+        mine_ref[at] = jnp.dot(plan[...], ext[at], preferred_element_type=jnp.float32).astype(mine_ref.dtype)
         moves.append(
             pltpu.make_async_remote_copy(
-                src_ref=moved.at[at], dst_ref=theirs_ref.at[at],
+                src_ref=mine_ref.at[at], dst_ref=theirs_ref.at[at],
                 send_sem=subj_send.at[c], recv_sem=subj_recv.at[c],
                 device_id={"subj": 1 - subj}, device_id_type=MESH,
             )
         )
-        moves.append(pltpu.make_async_copy(moved.at[at], mine_ref.at[at], mine_sem.at[c]))
-        for move in moves[-2:]:
-            move.start()
+        moves[-1].start()
+
+    @pl.when(is_byway)
+    def _():
+        for tile in DETOUR:
+            onward_copy(tile, slab).wait_send()
 
     for tile in range(tiles):
         norm_copy(tile).wait_send()
@@ -250,16 +319,19 @@
     rows = blocks * width
     tiles = blocks + PIECES
     dma = pltpu.SemaphoreType.DMA
-    anywhere = pl.BlockSpec(memory_space=pl.ANY)
+    hbm = pl.BlockSpec(memory_space=pltpu.HBM)
     vmem = pl.BlockSpec(memory_space=pltpu.VMEM)
     mine, theirs = pl.pallas_call(
         body,
         out_shape=[jax.ShapeDtypeStruct((rows, times), jnp.bfloat16)] * 2,
-        in_specs=[anywhere, anywhere, vmem, vmem],
-        out_specs=[anywhere, anywhere],
+        in_specs=[hbm] * 4,
+        out_specs=[vmem] * 2,
         scratch_shapes=[
             pltpu.VMEM((tiles * width, times), jnp.bfloat16),
             pltpu.VMEM((rows, times), jnp.bfloat16),
+            pltpu.VMEM(neighbours.shape, neighbours.dtype),
+            pltpu.VMEM(valid.shape, valid.dtype),
+            pltpu.VMEM((len(DETOUR), rows, width), jnp.int16),
             pltpu.VMEM((tiles, rows, width), jnp.float32),
             pltpu.VMEM((tiles, rows, width), jnp.int16),
             pltpu.VMEM((tiles, rows, width), jnp.int16),
@@ -267,17 +339,17 @@
             pltpu.VMEM((tiles, 8, width), jnp.float32),
             pltpu.VMEM((tiles, rows, width), jnp.float32),
             pltpu.VMEM((rows, tiles * width), jnp.bfloat16),
-            pltpu.VMEM((rows, times), jnp.bfloat16),
-            dma((2,)),
+            dma((4,)),
             dma((2 * PIECES,)), dma((2 * PIECES,)),
+            dma((len(DETOUR),)), dma((len(DETOUR),)),
             dma((tiles,)), dma((tiles,)),
             dma((tiles,)), dma((tiles,)),
-            dma((OUT_PIECES,)), dma((OUT_PIECES,)), dma((OUT_PIECES,)),
+            dma((OUT_PIECES,)), dma((OUT_PIECES,)),
         ],
         compiler_params=pltpu.CompilerParams(
             collective_id=0, has_side_effects=True, vmem_limit_bytes=32 * 2**20
         ),
-    )(subject_data.reshape(rows, times), template.reshape(rows, times), neighbours, valid)
+    )(*[pltpu.with_memory_space_constraint(x, pltpu.HBM) for x in (subject_data.reshape(rows, times), template.reshape(rows, times), neighbours, valid)])
     total = mine.astype(jnp.float32) + theirs.astype(jnp.float32)
     return total.astype(jnp.bfloat16).reshape(template.shape)
 

time: 41.4 us -> 36 us (0.87)
  local copies, waits for them, and re-layouts: 2.78 us -> 0 us
  Pallas kernels: 37.5 us -> 35 us
    unnamed x8 -> x0, local copies, waits for them, and re-layouts: 2.78 us -> none
    pallas_call x1, Pallas kernels: 37.5 us -> 35 us  [on_device(): pl.pallas_call(body, out_shape=[jax.ShapeDtypeStruct((rows, times), jnp.b...]
where the time goes in v3:
time: 36 us
  Pallas kernels  35 us (97%)
  other arithmetic  0.99 us (3%)
    pallas_call x1, Pallas kernels, on_device(): pl.pallas_call(body, out_shape=[jax.ShapeDtypeStruct((rows, times), jnp.b...  35 us
    convert_element_type x1, other arithmetic, on_device(): return total.astype(jnp.bfloat16).reshape(template.shape)  0.99 us

profile of v3, /device:TPU:25, one launch (start us, length us, event | category | flops | bytes accessed | tf_op | source)
XLA Modules:
  0.0 36.0 jit_solution(12023281944781159757)
XLA Ops:
  0.0 35.0 %shard_map.46 = (bf16[256,1024]{1,0:T(8,128)(2,1)S(1)}, bf16[256,1024]{1,0:T(8,128)(2,1)S(1)}) custom-call(bf16[256,1024]{1,0:T(8,128)(2,1)} %bitcast.3, bf16[256,1024]{1,0:T(8,128)(2,1)} %bitcast.4, s32[2,27]{1,0:T(2,128)} %near_ref.1, s32[2,27]{1,0:T(2,128)} %valid_ref.1), custom_call_target="tpu_custom_call" | custom-call | tf_op jit(solution)/shard_map/pallas_call | solution.py:324
  35.0 1.0 %add_convert_fusion = bf16[256,1024]{1,0:T(8,128)(2,1)} fusion(bf16[256,1024]{1,0:T(8,128)(2,1)S(1)} %get-tuple-element.8, bf16[256,1024]{1,0:T(8,128)(2,1)S(1)} %get-tuple-element.7), kind=kLoop, calls=%fused_computation | loop fusion | flops 1048576 | bytes 1572864 | tf_op jit(solution)/shard_map/convert_element_type | solution.py:354

commit v4 on v3

--- a/solution.py
+++ b/solution.py
@@ -251,16 +251,11 @@
     for tile in range(blocks):
         first_pass(tile)
     pass_on()
-    behind = 0
     for q in range(PIECES):
         arrived(q)
         first_pass(blocks + q)
-        while behind < blocks + q:
-            second_pass(behind)
-            behind += 1
-    while behind < tiles:
-        second_pass(behind)
-        behind += 1
+    for tile in range(tiles):
+        second_pass(tile)
 
     for b in range(blocks):
         at = pl.ds(b * width, width)

time: 36 us -> 32.6 us (0.906)
  Pallas kernels: 35 us -> 31.6 us
    pallas_call x1, Pallas kernels: 35 us -> 31.6 us  [on_device(): pl.pallas_call(body, out_shape=[jax.ShapeDtypeStruct((rows, times), jnp.b...]
where the time goes in v4:
time: 32.6 us; the launch traced here: 32.5 us
  Pallas kernels  31.6 us (97%)
  other arithmetic  0.99 us (3%)
    pallas_call x1, Pallas kernels, on_device(): pl.pallas_call(body, out_shape=[jax.ShapeDtypeStruct((rows, times), jnp.b...  31.6 us
    convert_element_type x1, other arithmetic, on_device(): return total.astype(jnp.bfloat16).reshape(template.shape)  0.99 us

profile of v4, /device:TPU:25, one launch (start us, length us, event | category | flops | bytes accessed | tf_op | source)
XLA Modules:
  0.0 32.5 jit_solution(5562139257241790262)
XLA Ops:
  0.0 31.6 %shard_map.46 = (bf16[256,1024]{1,0:T(8,128)(2,1)S(1)}, bf16[256,1024]{1,0:T(8,128)(2,1)S(1)}) custom-call(bf16[256,1024]{1,0:T(8,128)(2,1)} %bitcast.3, bf16[256,1024]{1,0:T(8,128)(2,1)} %bitcast.4, s32[2,27]{1,0:T(2,128)} %near_ref.1, s32[2,27]{1,0:T(2,128)} %valid_ref.1), custom_call_target="tpu_custom_call" | custom-call | tf_op jit(solution)/shard_map/pallas_call | solution.py:319
  31.6 1.0 %add_convert_fusion = bf16[256,1024]{1,0:T(8,128)(2,1)} fusion(bf16[256,1024]{1,0:T(8,128)(2,1)S(1)} %get-tuple-element.8, bf16[256,1024]{1,0:T(8,128)(2,1)S(1)} %get-tuple-element.7), kind=kLoop, calls=%fused_computation | loop fusion | flops 1048576 | bytes 1572864 | tf_op jit(solution)/shard_map/convert_element_type | solution.py:349

commit v5 on v4

v5 whole, which is shorter than its diff:
```python
import jax
import jax.numpy as jnp
from jax import lax
from jax.experimental import pallas as pl
from jax.experimental.pallas import tpu as pltpu
from jax.sharding import PartitionSpec as P

MESH = pl.DeviceIdType.MESH
ITERS = 3
SCALE = 32760.0
TINY = 1e-6
PIECES = (64, 64, 64, 32, 32)
RUN = 8
LOWER_DETOUR = (0, 1, 2, 3)
UPPER_DETOUR = (0, 1)
OUT_PIECES = 4


def times_transposed(a, b):
    return lax.dot_general(a, b, (((1,), (1,)), ((), ())), preferred_element_type=jnp.float32)


def body(
    data_ref, tmpl_ref, near_ref, valid_ref, mine_ref, theirs_ref,
    ext, tmpl, near, valid, passing, part, code_out, code_in, norm_out, norm_in, kern, plan,
    local_sem, slab_send, slab_recv, pass_send, pass_recv, code_send, code_recv, norm_send, norm_recv, subj_send, subj_recv, hello,
):
    slab, slabs = lax.axis_index("slab"), lax.axis_size("slab")
    subj, half = lax.axis_index("subj"), lax.axis_index("tm")
    rows, times = data_ref.shape
    width = 128
    blocks = rows // width
    columns = [width] * blocks + [2 * piece for piece in PIECES]
    tiles = len(columns)
    starts = [sum(columns[:tile]) for tile in range(tiles)]
    has_prev, has_next = slab > 0, slab < slabs - 1
    shared = (slabs // 2 - RUN, slabs // 2 + RUN - 1)
    routes = ((shared[0], 0, LOWER_DETOUR), (shared[1], shared[1] + RUN, UPPER_DETOUR))

    copies = [
        pltpu.make_async_copy(tmpl_ref, tmpl, local_sem.at[0]),
        pltpu.make_async_copy(data_ref, ext.at[pl.ds(0, rows)], local_sem.at[1]),
        pltpu.make_async_copy(near_ref, near, local_sem.at[2]),
        pltpu.make_async_copy(valid_ref, valid, local_sem.at[3]),
    ]
    for copy in copies:
        copy.start()

    barrier = pltpu.get_barrier_semaphore()

    def greet(where):
        pl.semaphore_signal(barrier, inc=1, device_id=where, device_id_type=MESH)

    greet({"subj": 1 - subj})

    @pl.when(half == 0)
    def _():
        greet({"tm": 1})

    @pl.when(has_prev)
    def _():
        greet({"slab": slab - 1})

    @pl.when(has_next)
    def _():
        greet({"slab": slab + 1})

    for crowded, way, _ in routes:

        @pl.when(slab == crowded)
        def _():
            greet({"slab": way, "tm": 1 - half})

        @pl.when(slab == way)
        def _():
            greet({"slab": crowded})

    greeted = (slab == shared[0]) | (slab == shared[1]) | (slab == routes[1][1])

    @pl.when(greeted)
    def _():
        pl.semaphore_wait(barrier, 4 + half)

    @pl.when(slab == slabs - 1)
    def _():
        pl.semaphore_wait(barrier, 2 + half)

    @pl.when(jnp.logical_not(greeted | (slab == slabs - 1)))
    def _():
        pl.semaphore_wait(barrier, 3 + half)

    @pl.when(half == 1)
    def _():
        pl.semaphore_signal(hello, inc=1, device_id={"tm": 0}, device_id_type=MESH)

    def slab_place(q, up):
        return pl.ds(starts[blocks + q] + (0 if up else PIECES[q]), PIECES[q])

    def slab_copy(q, up):
        k = q + (0 if up else len(PIECES))
        return pltpu.make_async_remote_copy(
            src_ref=data_ref.at[pl.ds(sum(PIECES[:q]), PIECES[q])],
            dst_ref=ext.at[slab_place(q, up)],
            send_sem=slab_send.at[k],
            recv_sem=slab_recv.at[k],
            device_id={"slab": slab + 1 if up else slab - 1},
            device_id_type=MESH,
        )

    for q in range(len(PIECES)):

        @pl.when(has_next)
        def _():
            slab_copy(q, True).start()

        @pl.when(has_prev)
        def _():
            slab_copy(q, False).start()

    for there, up in ((has_prev, True), (has_next, False)):

        @pl.when(jnp.logical_not(there))
        def _():
            for q, piece in enumerate(PIECES):
                ext[slab_place(q, up), :] = jnp.zeros((piece, times), ext.dtype)

    norm_out[...] = jnp.zeros(norm_out.shape, norm_out.dtype)

    copies[2].wait()
    copies[3].wait()
    seen = near[...] - (slab - 1) * blocks
    used = valid[...].astype(jnp.float32)
    count = [
        jnp.sum(jnp.where(seen == e, used, 0.0), axis=1, keepdims=True) for e in range(3 * blocks)
    ]
    goal = 1.0 / (width * jnp.sum(used, axis=1, keepdims=True))

    def counts(b, tile):
        if tile < blocks:
            return jnp.broadcast_to(count[blocks + tile][b : b + 1], (1, width))
        piece = PIECES[tile - blocks]
        owner = sum(PIECES[: tile - blocks]) // width
        lane = lax.broadcasted_iota(jnp.int32, (1, 2 * piece), 1)
        return jnp.where(lane < piece, count[owner][b : b + 1], count[2 * blocks + owner][b : b + 1])

    def diagonal(gram, axis):
        row, column = (lax.broadcasted_iota(jnp.int32, gram.shape, dim) for dim in (0, 1))
        return jnp.sum(jnp.where(row == column, gram, 0.0), axis=axis, keepdims=True)

    copies[0].wait()
    grams = [
        times_transposed(tmpl[pl.ds(b * width, width), :], tmpl[pl.ds(b * width, width), :])
        for b in range(blocks)
    ]
    row_sq = [diagonal(gram, 1) for gram in grams]
    row_unit = [lax.rsqrt(sq + TINY) * SCALE for sq in row_sq]

    def coded(tile):
        return pl.ds(0, rows * columns[tile] // width)

    def code_place(tile, b):
        beside = width // columns[tile]
        return (tile, pl.ds(b // beside * width, width), pl.ds(b % beside * columns[tile], columns[tile]))

    def code_copy(tile):
        return pltpu.make_async_remote_copy(
            src_ref=code_out.at[tile, coded(tile)], dst_ref=code_in.at[tile, coded(tile)],
            send_sem=code_send.at[tile], recv_sem=code_recv.at[tile],
            device_id={"tm": 1 - half}, device_id_type=MESH,
        )

    def detour_copy(tile, way):
        return pltpu.make_async_remote_copy(
            src_ref=code_out.at[tile, coded(tile)], dst_ref=passing.at[tile, coded(tile)],
            send_sem=code_send.at[tile], recv_sem=pass_recv.at[tile],
            device_id={"slab": way}, device_id_type=MESH,
        )

    def onward_copy(tile, crowded):
        return pltpu.make_async_remote_copy(
            src_ref=passing.at[tile, coded(tile)], dst_ref=code_in.at[tile, coded(tile)],
            send_sem=pass_send.at[tile], recv_sem=code_recv.at[tile],
            device_id={"slab": crowded, "tm": 1 - half}, device_id_type=MESH,
        )

    def send_code(tile):
        ways = [(crowded, way) for crowded, way, taking in routes if tile in taking]
        direct = jnp.bool_(True)
        for crowded, way in ways:
            direct &= slab != crowded

            @pl.when(slab == crowded)
            def _():
                detour_copy(tile, way).start()

        if not ways:
            code_copy(tile).start()
            return

        @pl.when(direct)
        def _():
            code_copy(tile).start()

    def pass_on(route, turn):
        for crowded, way, taking in routes[route : route + 1]:

            @pl.when(slab == way)
            def _():
                for tile in turn:
                    if tile in taking:
                        detour_copy(tile, way).wait_recv()
                        onward_copy(tile, crowded).start()

    def norm_copy(tile):
        return pltpu.make_async_remote_copy(
            src_ref=norm_out.at[tile], dst_ref=norm_in.at[tile],
            send_sem=norm_send.at[tile], recv_sem=norm_recv.at[tile],
            device_id={"tm": 1 - half}, device_id_type=MESH,
        )

    def first_pass(tile):
        data = ext[pl.ds(starts[tile], columns[tile]), :]
        wide = pl.ds(0, columns[tile])
        col_sq = diagonal(times_transposed(data, data), 0)
        norm_out[tile, 0:1, wide] = col_sq
        if tile == 0:
            for b in range(blocks):
                norm_out[tile, 1 + b : 2 + b, :] = diagonal(grams[b], 0)
        col_unit = lax.rsqrt(col_sq + TINY)
        for b in range(blocks):
            at = pl.ds(b * width, width)
            cross = times_transposed(tmpl[at, :], data)
            part[tile, at, wide] = cross
            code_out[code_place(tile, b)] = jnp.round(cross * row_unit[b] * col_unit).astype(jnp.int32).astype(jnp.int16)

    def send(tile):
        norm_copy(tile).start()
        send_code(tile)

    scales = {}

    def second_pass(tile):
        norm_copy(tile).wait_recv()
        wide = pl.ds(0, columns[tile])
        if tile == 0:
            for b in range(blocks):
                row, column = (lax.broadcasted_iota(jnp.int32, (width, width), dim) for dim in (0, 1))
                other = jnp.sum(
                    jnp.where(row == column, norm_in[tile, 1 + b : 2 + b, :], 0.0), axis=1, keepdims=True
                )
                row_scale = lax.rsqrt(row_sq[b] + other + 1e-6)
                scales[b] = (row_scale, row_scale * ((other + TINY) * lax.rsqrt(other + TINY)))
        col_sq = norm_out[tile, 0:1, wide]
        other = norm_in[tile, 0:1, wide]
        col_scale = lax.rsqrt(col_sq + other + 1e-6) * (1.0 / 0.03)
        col_other = col_scale * ((other + TINY) * lax.rsqrt(other + TINY)) * (1.0 / SCALE)
        code_copy(tile).wait_recv()
        for b in range(blocks):
            at = pl.ds(b * width, width)
            logits = part[tile, at, wide] * (scales[b][0] * col_scale)
            logits += code_in[code_place(tile, b)].astype(jnp.int32).astype(jnp.float32) * (scales[b][1] * col_other)
            kern[tile, at, wide] = jnp.exp(logits)

    def arrived(q):
        @pl.when(has_prev)
        def _():
            slab_copy(q, True).wait_recv()

        @pl.when(has_next)
        def _():
            slab_copy(q, False).wait_recv()

    copies[1].wait()
    for tile in range(blocks):
        first_pass(tile)

    @pl.when(half == 0)
    def _():
        pl.semaphore_wait(hello, 1)

    for tile in range(blocks):
        send(tile)
    pass_on(1, UPPER_DETOUR)
    for q in range(len(PIECES)):
        arrived(q)
        first_pass(blocks + q)
        send(blocks + q)
        if q == 1:
            pass_on(0, [tile for tile in LOWER_DETOUR if tile < blocks])
    pass_on(0, [tile for tile in LOWER_DETOUR if tile >= blocks])
    for tile in range(tiles):
        second_pass(tile)

    for b in range(blocks):
        at = pl.ds(b * width, width)
        number = [counts(b, tile) for tile in range(tiles)]
        weight = number

        def flow(tile, w):
            return kern[tile, at, pl.ds(0, columns[tile])] * w

        def row_sums(weight):
            whole = sum(flow(tile, weight[tile]) for tile in range(tiles) if columns[tile] == width)
            sums = jnp.sum(whole, axis=1, keepdims=True)
            rest = [flow(tile, weight[tile]) for tile in range(tiles) if columns[tile] < width]
            return sums + jnp.sum(sum(rest), axis=1, keepdims=True) if rest else sums

        for _ in range(ITERS):
            row_weight = (1.0 / width) / row_sums(weight)
            weight = [
                number[tile] * goal[b : b + 1] / jnp.sum(flow(tile, row_weight), axis=0, keepdims=True)
                for tile in range(tiles)
            ]
        share = 0.5 / row_sums(weight)
        for tile in range(tiles):
            plan[at, pl.ds(starts[tile], columns[tile])] = (flow(tile, weight[tile]) * share).astype(plan.dtype)

    wide = times // OUT_PIECES
    moves = []
    for c in range(OUT_PIECES):
        at = (slice(None), pl.ds(c * wide, wide))
        mine_ref[at] = jnp.dot(plan[...], ext[at], preferred_element_type=jnp.float32).astype(mine_ref.dtype)
        moves.append(
            pltpu.make_async_remote_copy(
                src_ref=mine_ref.at[at], dst_ref=theirs_ref.at[at],
                send_sem=subj_send.at[c], recv_sem=subj_recv.at[c],
                device_id={"subj": 1 - subj}, device_id_type=MESH,
            )
        )
        moves[-1].start()

    for crowded, way, taking in routes:

        @pl.when(slab == way)
        def _():
            for tile in taking:
                onward_copy(tile, crowded).wait_send()

    for tile in range(tiles):
        norm_copy(tile).wait_send()
        code_copy(tile).wait_send()
    for q in range(len(PIECES)):

        @pl.when(has_next)
        def _():
            slab_copy(q, True).wait_send()

        @pl.when(has_prev)
        def _():
            slab_copy(q, False).wait_send()

    for move in moves:
        move.wait()


def on_device(subject_data, template, neighbours, valid):
    _, blocks, width, times = subject_data.shape
    rows = blocks * width
    pieces, tiles = len(PIECES), blocks + len(PIECES)
    detours = max(LOWER_DETOUR + UPPER_DETOUR) + 1
    dma = pltpu.SemaphoreType.DMA
    hbm = pl.BlockSpec(memory_space=pltpu.HBM)
    vmem = pl.BlockSpec(memory_space=pltpu.VMEM)
    mine, theirs = pl.pallas_call(
        body,
        out_shape=[jax.ShapeDtypeStruct((rows, times), jnp.bfloat16)] * 2,
        in_specs=[hbm] * 4,
        out_specs=[vmem] * 2,
        scratch_shapes=[
            pltpu.VMEM((3 * rows, times), jnp.bfloat16),
            pltpu.VMEM((rows, times), jnp.bfloat16),
            pltpu.VMEM(neighbours.shape, neighbours.dtype),
            pltpu.VMEM(valid.shape, valid.dtype),
            pltpu.VMEM((detours, rows, width), jnp.int16),
            pltpu.VMEM((tiles, rows, width), jnp.float32),
            pltpu.VMEM((tiles, rows, width), jnp.int16),
            pltpu.VMEM((tiles, rows, width), jnp.int16),
            pltpu.VMEM((tiles, 8, width), jnp.float32),
            pltpu.VMEM((tiles, 8, width), jnp.float32),
            pltpu.VMEM((tiles, rows, width), jnp.float32),
            pltpu.VMEM((rows, 3 * rows), jnp.bfloat16),
            dma((4,)),
            dma((2 * pieces,)), dma((2 * pieces,)),
            dma((detours,)), dma((detours,)),
            dma((tiles,)), dma((tiles,)),
            dma((tiles,)), dma((tiles,)),
            dma((OUT_PIECES,)), dma((OUT_PIECES,)),
            pltpu.SemaphoreType.REGULAR,
        ],
        compiler_params=pltpu.CompilerParams(
            collective_id=0, has_side_effects=True, vmem_limit_bytes=32 * 2**20
        ),
    )(*[pltpu.with_memory_space_constraint(x, pltpu.HBM) for x in (subject_data.reshape(rows, times), template.reshape(rows, times), neighbours, valid)])
    total = mine.astype(jnp.float32) + theirs.astype(jnp.float32)
    return total.astype(jnp.bfloat16).reshape(template.shape)


def solution(mesh):
    placed = (
        P("subj", "slab", None, "tm"),
        P("slab", None, "tm"),
        P("slab", None),
        P("slab", None),
    )
    return jax.shard_map(
        on_device, mesh=mesh, in_specs=placed, out_specs=P("slab", None, "tm"), check_vma=False
    )
```

time: 32.6 us -> 31.3 us (0.960)
  the two profiles are of different devices: /device:TPU:25 before, /device:TPU:3 now
where the time goes in v5:
time: 31.3 us
  Pallas kernels  30.3 us (97%)
  other arithmetic  0.99 us (3%)
    pallas_call x1, Pallas kernels, on_device(): pl.pallas_call(body, out_shape=[jax.ShapeDtypeStruct((rows, times), jnp.b...  30.3 us
    convert_element_type x1, other arithmetic, on_device(): return total.astype(jnp.bfloat16).reshape(template.shape)  0.99 us

profile of v5, /device:TPU:3, one launch (start us, length us, event | category | flops | bytes accessed | tf_op | source)
XLA Modules:
  0.0 31.3 jit_solution(14325420050038420902)
XLA Ops:
  0.0 30.3 %shard_map.46 = (bf16[256,1024]{1,0:T(8,128)(2,1)S(1)}, bf16[256,1024]{1,0:T(8,128)(2,1)S(1)}) custom-call(bf16[256,1024]{1,0:T(8,128)(2,1)} %bitcast.3, bf16[256,1024]{1,0:T(8,128)(2,1)} %bitcast.4, s32[2,27]{1,0:T(2,128)} %near_ref.1, s32[2,27]{1,0:T(2,128)} %valid_ref.1), custom_call_target="tpu_custom_call" | custom-call | tf_op jit(solution)/shard_map/pallas_call | solution.py:364
  30.3 1.0 %add_convert_fusion = bf16[256,1024]{1,0:T(8,128)(2,1)} fusion(bf16[256,1024]{1,0:T(8,128)(2,1)S(1)} %get-tuple-element.8, bf16[256,1024]{1,0:T(8,128)(2,1)S(1)} %get-tuple-element.7), kind=kLoop, calls=%fused_computation | loop fusion | flops 1048576 | bytes 1572864 | tf_op jit(solution)/shard_map/convert_element_type | solution.py:395

commit v6 on v5

--- a/solution.py
+++ b/solution.py
@@ -11,9 +11,8 @@
 TINY = 1e-6
 PIECES = (64, 64, 64, 32, 32)
 RUN = 8
-LOWER_DETOUR = (0, 1, 2, 3)
-UPPER_DETOUR = (0, 1)
-OUT_PIECES = 4
+DETOUR = (0, 1, 2)
+OUT_PIECES = 2
 
 
 def times_transposed(a, b):
@@ -34,8 +33,7 @@
     tiles = len(columns)
     starts = [sum(columns[:tile]) for tile in range(tiles)]
     has_prev, has_next = slab > 0, slab < slabs - 1
-    shared = (slabs // 2 - RUN, slabs // 2 + RUN - 1)
-    routes = ((shared[0], 0, LOWER_DETOUR), (shared[1], shared[1] + RUN, UPPER_DETOUR))
+    lower, upper = routes = ((slabs // 2 - RUN, 0), (slabs // 2 + RUN - 1, slabs - 1))
 
     copies = [
         pltpu.make_async_copy(tmpl_ref, tmpl, local_sem.at[0]),
@@ -51,7 +49,9 @@
     def greet(where):
         pl.semaphore_signal(barrier, inc=1, device_id=where, device_id_type=MESH)
 
-    greet({"subj": 1 - subj})
+    @pl.when(subj == 1)
+    def _():
+        greet({"subj": 0})
 
     @pl.when(half == 0)
     def _():
@@ -61,37 +61,51 @@
     def _():
         greet({"slab": slab - 1})
 
+    @pl.when(slab == lower[0])
+    def _():
+        greet({"slab": lower[1], "tm": 1 - half})
+
+    @pl.when(slab == lower[1])
+    def _():
+        greet({"slab": lower[0]})
+
+    @pl.when(slab == upper[0])
+    def _():
+        greet({"slab": upper[1]})
+        greet({"slab": upper[1], "tm": 1 - half})
+
+    on_lower = (slab == lower[0]) | (slab == lower[1])
+
+    @pl.when(on_lower)
+    def _():
+        pl.semaphore_wait(barrier, 3 - subj + half)
+
+    @pl.when(slab == upper[1])
+    def _():
+        pl.semaphore_wait(barrier, 3 - subj + half)
+
+    @pl.when(jnp.logical_not(on_lower | (slab == upper[1])))
+    def _():
+        pl.semaphore_wait(barrier, 2 - subj + half)
+
+    def hail(k, where):
+        pl.semaphore_signal(hello.at[k], inc=1, device_id=where, device_id_type=MESH)
+
     @pl.when(has_next)
     def _():
-        greet({"slab": slab + 1})
-
-    for crowded, way, _ in routes:
-
-        @pl.when(slab == crowded)
-        def _():
-            greet({"slab": way, "tm": 1 - half})
-
-        @pl.when(slab == way)
-        def _():
-            greet({"slab": crowded})
-
-    greeted = (slab == shared[0]) | (slab == shared[1]) | (slab == routes[1][1])
-
-    @pl.when(greeted)
-    def _():
-        pl.semaphore_wait(barrier, 4 + half)
-
-    @pl.when(slab == slabs - 1)
-    def _():
-        pl.semaphore_wait(barrier, 2 + half)
-
-    @pl.when(jnp.logical_not(greeted | (slab == slabs - 1)))
-    def _():
-        pl.semaphore_wait(barrier, 3 + half)
+        hail(0, {"slab": slab + 1})
+
+    @pl.when(subj == 0)
+    def _():
+        hail(1, {"subj": 1})
 
     @pl.when(half == 1)
     def _():
-        pl.semaphore_signal(hello, inc=1, device_id={"tm": 0}, device_id_type=MESH)
+        hail(2, {"tm": 0})
+
+    @pl.when(slab == upper[1])
+    def _():
+        hail(3, {"slab": upper[0]})
 
     def slab_place(q, up):
         return pl.ds(starts[blocks + q] + (0 if up else PIECES[q]), PIECES[q])
@@ -113,10 +127,6 @@
         def _():
             slab_copy(q, True).start()
 
-        @pl.when(has_prev)
-        def _():
-            slab_copy(q, False).start()
-
     for there, up in ((has_prev, True), (has_next, False)):
 
         @pl.when(jnp.logical_not(there))
@@ -184,32 +194,28 @@
         )
 
     def send_code(tile):
-        ways = [(crowded, way) for crowded, way, taking in routes if tile in taking]
-        direct = jnp.bool_(True)
-        for crowded, way in ways:
-            direct &= slab != crowded
+        if tile not in DETOUR:
+            code_copy(tile).start()
+            return
+
+        for crowded, way in routes:
 
             @pl.when(slab == crowded)
             def _():
                 detour_copy(tile, way).start()
 
-        if not ways:
+        @pl.when((slab != lower[0]) & (slab != upper[0]))
+        def _():
             code_copy(tile).start()
-            return
-
-        @pl.when(direct)
-        def _():
-            code_copy(tile).start()
-
-    def pass_on(route, turn):
-        for crowded, way, taking in routes[route : route + 1]:
+
+    def pass_on(turn):
+        for crowded, way in routes:
 
             @pl.when(slab == way)
             def _():
                 for tile in turn:
-                    if tile in taking:
-                        detour_copy(tile, way).wait_recv()
-                        onward_copy(tile, crowded).start()
+                    detour_copy(tile, way).wait_recv()
+                    onward_copy(tile, crowded).start()
 
     def norm_copy(tile):
         return pltpu.make_async_remote_copy(
@@ -274,20 +280,29 @@
     for tile in range(blocks):
         first_pass(tile)
 
+    @pl.when(has_prev)
+    def _():
+        pl.semaphore_wait(hello.at[0], 1)
+        for q in range(len(PIECES)):
+            slab_copy(q, False).start()
+
     @pl.when(half == 0)
     def _():
-        pl.semaphore_wait(hello, 1)
+        pl.semaphore_wait(hello.at[2], 1)
+
+    @pl.when(slab == upper[0])
+    def _():
+        pl.semaphore_wait(hello.at[3], 1)
 
     for tile in range(blocks):
         send(tile)
-    pass_on(1, UPPER_DETOUR)
     for q in range(len(PIECES)):
         arrived(q)
         first_pass(blocks + q)
         send(blocks + q)
         if q == 1:
-            pass_on(0, [tile for tile in LOWER_DETOUR if tile < blocks])
-    pass_on(0, [tile for tile in LOWER_DETOUR if tile >= blocks])
+            pass_on([tile for tile in DETOUR if tile < blocks])
+    pass_on([tile for tile in DETOUR if tile >= blocks])
     for tile in range(tiles):
         second_pass(tile)
 
@@ -314,6 +329,10 @@
         share = 0.5 / row_sums(weight)
         for tile in range(tiles):
             plan[at, pl.ds(starts[tile], columns[tile])] = (flow(tile, weight[tile]) * share).astype(plan.dtype)
+
+    @pl.when(subj == 1)
+    def _():
+        pl.semaphore_wait(hello.at[1], 1)
 
     wide = times // OUT_PIECES
     moves = []
@@ -329,11 +348,11 @@
         )
         moves[-1].start()
 
-    for crowded, way, taking in routes:
+    for crowded, way in routes:
 
         @pl.when(slab == way)
         def _():
-            for tile in taking:
+            for tile in DETOUR:
                 onward_copy(tile, crowded).wait_send()
 
     for tile in range(tiles):
@@ -357,7 +376,7 @@
     _, blocks, width, times = subject_data.shape
     rows = blocks * width
     pieces, tiles = len(PIECES), blocks + len(PIECES)
-    detours = max(LOWER_DETOUR + UPPER_DETOUR) + 1
+    detours = len(DETOUR)
     dma = pltpu.SemaphoreType.DMA
     hbm = pl.BlockSpec(memory_space=pltpu.HBM)
     vmem = pl.BlockSpec(memory_space=pltpu.VMEM)
@@ -385,7 +404,7 @@
             dma((tiles,)), dma((tiles,)),
             dma((tiles,)), dma((tiles,)),
             dma((OUT_PIECES,)), dma((OUT_PIECES,)),
-            pltpu.SemaphoreType.REGULAR,
+            pltpu.SemaphoreType.REGULAR((4,)),
         ],
         compiler_params=pltpu.CompilerParams(
             collective_id=0, has_side_effects=True, vmem_limit_bytes=32 * 2**20

time: 31.3 us -> 30.7 us (0.981)
  the two profiles are of different devices: /device:TPU:3 before, /device:TPU:25 now
where the time goes in v6:
time: 30.7 us; the launch traced here: 30.6 us
  Pallas kernels  29.6 us (96%)
  other arithmetic  0.99 us (3%)
    pallas_call x1, Pallas kernels, on_device(): pl.pallas_call(body, out_shape=[jax.ShapeDtypeStruct((rows, times), jnp.b...  29.6 us
    convert_element_type x1, other arithmetic, on_device(): return total.astype(jnp.bfloat16).reshape(template.shape)  0.99 us

profile of v6, /device:TPU:25, one launch (start us, length us, event | category | flops | bytes accessed | tf_op | source)
XLA Modules:
  0.0 30.6 jit_solution(11530946723678019512)
XLA Ops:
  0.0 29.6 %shard_map.46 = (bf16[256,1024]{1,0:T(8,128)(2,1)S(1)}, bf16[256,1024]{1,0:T(8,128)(2,1)S(1)}) custom-call(bf16[256,1024]{1,0:T(8,128)(2,1)} %bitcast.3, bf16[256,1024]{1,0:T(8,128)(2,1)} %bitcast.4, s32[2,27]{1,0:T(2,128)} %near_ref.1, s32[2,27]{1,0:T(2,128)} %valid_ref.1), custom_call_target="tpu_custom_call" | custom-call | tf_op jit(solution)/shard_map/pallas_call | solution.py:383
  29.6 1.0 %add_convert_fusion = bf16[256,1024]{1,0:T(8,128)(2,1)} fusion(bf16[256,1024]{1,0:T(8,128)(2,1)S(1)} %get-tuple-element.8, bf16[256,1024]{1,0:T(8,128)(2,1)S(1)} %get-tuple-element.7), kind=kLoop, calls=%fused_computation | loop fusion | flops 1048576 | bytes 1572864 | tf_op jit(solution)/shard_map/convert_element_type | solution.py:414
